TPU v7x, 32 devices: a whole 2x2x4 slice. The times are simulated.
32 devices in a mesh: gx: 4 (over y, x), gy: 2 (over core), gz: 4 (over z).
Axes of the slice: x: 2, y: 2, z: 4, core: 2. Of those that a mesh axis runs over, the one named last changes fastest.
Arguments:
- panel: float32 [4, 2, 16, 256, 256], P('gx', 'gy', 'gz'), may hold values from -120 to 120
- tiles: float32 [4, 2, 16, 10, 256, 256], P('gx', 'gy', 'gz'), may hold values from -0.125 to 0.125
- codes: int32 [4, 2, 16, 10], P('gx', 'gy', 'gz'), may hold values from 0 to 26, as said below
Outputs:
- bands: float32 [4, 2, 16, 256, 256], P('gx', 'gy', 'gz')
- factor: float32 [256, 256], replicated
Inputs may be any that keep to these rules, and one draw needn't show every extreme that they name: Slot 0 of every element holds 13, the element itself; the other 9 slots of an element hold distinct codes other than 13.
All inputs are finite; a program needn't handle non-finite values.
Results may differ from a plain program's by a relative error of at most 0.0003.
Values sent between devices are 32-bit elements; how exact they have to be, the bound alone decides.
A program may use at most 128 MiB of HBM per device.

v0:
```python
import jax
import jax.numpy as jnp
from jax import lax
from jax.sharding import PartitionSpec as P


def padded_2(shard, sides, width):
    for axis, dim in sides:
        peers, length = (lax.axis_size(axis), shard.shape[dim])
        up = [(i, (i + 1) % peers) for i in range(peers - 1)]
        down = [(j, i) for i, j in up]
        last = lax.slice_in_dim(shard, length - width, length, axis=dim)
        initial = lax.slice_in_dim(shard, 0, width, axis=dim)
        before = lax.ppermute(last, axis, up)
        after = lax.ppermute(initial, axis, down)
        shard = jnp.concatenate([before, shard, after], axis=dim)
    return shard


def window(padded, first, second, third):
    zero = jnp.zeros((), jnp.int32)
    piece = lax.dynamic_slice(
        padded, (first, second, third, zero, zero), (1, 1, 1, padded.shape[3], padded.shape[4])
    )
    return piece[0, 0, 0]


def per_device(panel, tiles, codes):
    along_x = padded_2(panel, (("gx", 0),), 1)
    along_y = padded_2(along_x, (("gy", 1),), 1)
    padded = padded_2(along_y, (("gz", 2),), 1)
    width = panel.shape[4]
    products = []
    for element_cell in range(panel.shape[2]):
        slot_codes = codes[0, 0, element_cell]
        windows = jax.vmap(lambda c: window(padded, c // 9, c // 3 % 3, element_cell + c % 3))(
            slot_codes
        )
        applied = jnp.einsum(
            "kab,kbc->ac", tiles[0, 0, element_cell], windows, precision=lax.Precision.HIGHEST
        )
        products.append(applied - 0.5 * panel[0, 0, element_cell])
    filtered = jnp.stack(products)
    flat_rows = filtered.reshape(-1, width)
    local_gram = jnp.dot(flat_rows.T, flat_rows, precision=lax.Precision.HIGHEST)
    row_total = flat_rows.shape[0] * lax.axis_size("gx") * lax.axis_size("gy") * lax.axis_size("gz")
    gram_part = lax.psum_scatter(local_gram, "gz", scatter_dimension=0, tiled=True)
    gram_part = lax.psum(gram_part, ("gx", "gy"))
    summed = lax.all_gather(gram_part, "gz", axis=0, tiled=True)
    gram = summed / row_total
    lower = jnp.linalg.cholesky(gram)
    inverse = lax.linalg.triangular_solve(
        lower, jnp.eye(width, dtype=gram.dtype), left_side=True, lower=True
    )
    bands = jnp.dot(flat_rows, inverse.T, precision=lax.Precision.HIGHEST).reshape(panel.shape)
    return (bands, lower.T)


def solution(mesh):
    in_specs = (
        P("gx", "gy", "gz", None, None),
        P("gx", "gy", "gz", None, None, None),
        P("gx", "gy", "gz", None),
    )
    out_specs = (P("gx", "gy", "gz", None, None), P())
    return jax.shard_map(
        per_device, mesh=mesh, in_specs=in_specs, out_specs=out_specs, check_vma=False
    )
```

profile of v0, /device:TPU:0, one launch (start us, length us, event | category | flops | bytes accessed | tf_op | source)
XLA Modules:
  0.0 357.0 jit_solution(12483435723269355721)
XLA Ops:
  7.2 5.1 %collective-permute-start = (f32[1,1,4,256,256]{4,3,2,1,0:T(8,128)}, f32[1,1,4,256,256]{4,3,2,1,0:T(8,128)S(1)}, u32[]{:S(2)}, u32[]{:S(2)}) collective-permute-start(f32[1,1,4,256,256]{4,3,2,1,0:T(8,128)} %param.3), channel_id=1, source_target_pairs={{0,8},{8,16},{16,24},{1,9},{9,17},{17,25},{2,10},{10,18},{18,26},{... | collective-permute-start | bytes 3145736 | tf_op jit(solution)/shard_map/ppermute | solution.py:14
  12.3 1.3 collective-permute-start.1
  13.6 21.3 %collective-permute-done = f32[1,1,4,256,256]{4,3,2,1,0:T(8,128)S(1)} collective-permute-done((f32[1,1,4,256,256]{4,3,2,1,0:T(8,128)}, f32[1,1,4,256,256]{4,3,2,1,0:T(8,128)S(1)}, u32[]{:S(2)}, u32[]{:S(2)}) %collective-permute-start) | collective-permute-done | bytes 1048608 | tf_op jit(solution)/shard_map/ppermute | solution.py:14
  35.1 24.1 %collective-permute-done.1 = f32[1,1,4,256,256]{4,3,2,1,0:T(8,128)S(1)} collective-permute-done((f32[1,1,4,256,256]{4,3,2,1,0:T(8,128)}, f32[1,1,4,256,256]{4,3,2,1,0:T(8,128)S(1)}, u32[]{:S(2)}, u32[]{:S(2)}) %collective-permute-start.1) | collective-permute-done | bytes 1048608 | tf_op jit(solution)/shard_map/ppermute | solution.py:15
  59.3 1.5 collective-permute-start.2
  60.8 1.3 collective-permute-start.3
  62.1 3.8 %collective-permute-done.2 = f32[3,1,4,256,256]{4,3,2,1,0:T(8,128)S(1)} collective-permute-done((f32[3,1,4,256,256]{4,3,2,1,0:T(8,128)S(1)}, f32[3,1,4,256,256]{4,3,2,1,0:T(8,128)S(1)}, u32[]{:S(2)}, u32[]{:S(2)}) %collective-permute-start.2) | collective-permute-done | bytes 3145760 | tf_op jit(solution)/shard_map/ppermute | solution.py:14
  65.9 2.5 collective-permute-done.3
  68.4 2.8 pad_maximum_fusion.3
  71.4 5.0 %collective-permute-start.4 = (f32[3,3,1,256,256]{4,3,2,1,0:T(8,128)}, f32[3,3,1,256,256]{4,3,2,1,0:T(8,128)}, u32[]{:S(2)}, u32[]{:S(2)}) collective-permute-start(f32[3,3,1,256,256]{4,3,2,1,0:T(8,128)} %get-tuple-element.24), channel_id=1, source_target_pairs={{0,1},{1,2},{2,3},{4,5},{5,6},{6,7},{8,9},{9,10},{10,11},{12,13},{... | collective-permute-start | bytes 7077896 | tf_op jit(solution)/shard_map/ppermute | solution.py:14
  76.4 1.3 collective-permute-start.5
  77.7 0.9 fusion.104
  78.6 0.9 copy.46
  79.5 1.1 copy.45
  80.6 1.8 copy.44
  82.4 1.8 copy.43
  84.2 41.9 %collective-permute-done.4 = f32[3,3,1,256,256]{4,3,2,1,0:T(8,128)} collective-permute-done((f32[3,3,1,256,256]{4,3,2,1,0:T(8,128)}, f32[3,3,1,256,256]{4,3,2,1,0:T(8,128)}, u32[]{:S(2)}, u32[]{:S(2)}) %collective-permute-start.4) | collective-permute-done | bytes 2359328 | tf_op jit(solution)/shard_map/ppermute | solution.py:14
  126.1 5.5 %collective-permute-done.5 = f32[3,3,1,256,256]{4,3,2,1,0:T(8,128)} collective-permute-done((f32[3,3,1,256,256]{4,3,2,1,0:T(8,128)}, f32[3,3,1,256,256]{4,3,2,1,0:T(8,128)}, u32[]{:S(2)}, u32[]{:S(2)}) %collective-permute-start.5) | collective-permute-done | bytes 2359328 | tf_op jit(solution)/shard_map/ppermute | solution.py:15
  131.7 9.7 %pad_maximum_fusion = f32[3,3,6,256,256]{4,3,2,1,0:T(8,128)} fusion(f32[3,3,1,256,256]{4,3,2,1,0:T(8,128)} %collective-permute-done.5, f32[3,1,4,256,256]{4,3,2,1,0:T(8,128)} %copy-done.1, f32[3,1,4,256,256]{4,3,2,1,0:T(8,128)S(1)} %constant_dynamic-update-slice_fusion, f32[3,1,4,256,256]{4,3,2,1,0:T(8,128)} %copy-done, ...), kind=kLoop, calls=%fused_computation.6 | loop fusion | flops 14155776 | bytes 28311552 | tf_op jit(solution)/shard_map/concatenate | solution.py:16
  141.3 7.3 %gather_fusion.3 = f32[10,256,256]{2,1,0:T(8,128)} fusion(f32[3,3,6,256,256]{4,3,2,1,0:T(8,128)} %pad_maximum_fusion, s32[10]{0:T(128)S(1)} %get-tuple-element.38), kind=kCustom, calls=%fused_computation.3 | custom fusion | bytes 5243080 | tf_op jit(solution)/shard_map/vmap()/gather | solution.py:22
  148.6 7.4 %gather_fusion.2 = f32[10,256,256]{2,1,0:T(8,128)} fusion(f32[3,3,6,256,256]{4,3,2,1,0:T(8,128)} %pad_maximum_fusion, s32[10]{0:T(128)S(1)} %get-tuple-element.39), kind=kCustom, calls=%fused_computation.2 | custom fusion | bytes 5243080 | tf_op jit(solution)/shard_map/vmap()/gather | solution.py:22
  156.0 5.7 %gather_fusion.1 = f32[10,256,256]{2,1,0:T(8,128)S(1)} fusion(f32[3,3,6,256,256]{4,3,2,1,0:T(8,128)} %pad_maximum_fusion, s32[10]{0:T(128)S(1)} %get-tuple-element.37), kind=kCustom, calls=%fused_computation.1 | custom fusion | bytes 5243080 | tf_op jit(solution)/shard_map/vmap()/gather | solution.py:22
  161.8 7.4 %gather_fusion = f32[10,256,256]{2,1,0:T(8,128)} fusion(f32[3,3,6,256,256]{4,3,2,1,0:T(8,128)} %pad_maximum_fusion, s32[10]{0:T(128)S(1)} %get-tuple-element.36), kind=kCustom, calls=%fused_computation | custom fusion | bytes 5243080 | tf_op jit(solution)/shard_map/vmap()/gather | solution.py:22
  169.2 7.0 %fusion.27 = f32[1,256,256]{1,2,0:T(8,128)S(1)} fusion(f32[10,256,256]{2,1,0:T(8,128)} %gather_fusion.3, f32[1,1,4,10,256,256]{5,4,3,2,1,0:T(8,128)} %param.4, f32[1,1,1,256,256]{3,4,2,1,0:T(8,128)S(1)} %copy-done.7), kind=kOutput, calls=%fused_computation.29 | convolution fusion | flops 2013396992 | bytes 5767168 | tf_op jit(solution)/shard_map/kab,kbc->ac/dot_general | solution.py:39
  176.1 6.2 %fusion.33 = f32[1,256,256]{1,2,0:T(8,128)S(1)} fusion(f32[10,256,256]{2,1,0:T(8,128)S(1)} %copy-done.3, f32[1,1,4,10,256,256]{5,4,3,2,1,0:T(8,128)} %param.4, f32[1,1,1,256,256]{3,4,2,1,0:T(8,128)S(1)} %copy.45), kind=kOutput, calls=%fused_computation.31 | convolution fusion | flops 2013396992 | bytes 5767168 | tf_op jit(solution)/shard_map/kab,kbc->ac/dot_general | solution.py:39
  182.4 6.7 %fusion.39 = f32[1,256,256]{1,2,0:T(8,128)S(1)} fusion(f32[10,256,256]{2,1,0:T(8,128)S(1)} %gather_fusion.1, f32[1,1,4,10,256,256]{5,4,3,2,1,0:T(8,128)} %param.4, f32[1,1,1,256,256]{3,4,2,1,0:T(8,128)S(1)} %copy-done.5), kind=kOutput, calls=%fused_computation.33 | convolution fusion | flops 2013396992 | bytes 5767168 | tf_op jit(solution)/shard_map/kab,kbc->ac/dot_general | solution.py:39
  189.1 6.2 %fusion.45 = f32[1,256,256]{1,2,0:T(8,128)S(1)} fusion(f32[10,256,256]{2,1,0:T(8,128)S(1)} %copy-done.2, f32[1,1,4,10,256,256]{5,4,3,2,1,0:T(8,128)} %param.4, f32[1,1,1,256,256]{3,4,2,1,0:T(8,128)S(1)} %copy-done.6), kind=kOutput, calls=%fused_computation.35 | convolution fusion | flops 2013396992 | bytes 5767168 | tf_op jit(solution)/shard_map/kab,kbc->ac/dot_general | solution.py:39
  195.4 1.7 convolution_bitcast_fusion.1
  197.2 18.0 %reduce-scatter.4.cloned.1.call-done = f32[64,256]{1,0:T(8,128)} async-done(((f32[256,256]{1,0:T(8,128)}), f32[64,256]{1,0:T(8,128)}) %reduce-scatter.4.cloned.1.call-update) | async-done | bytes 65552
  215.2 1.6 copy.42
  216.8 53.7 %all-reduce.3.cloned.1.call-done = f32[64,256]{0,1:T(8,128)} async-done(((f32[64,256]{0,1:T(8,128)}), f32[64,256]{0,1:T(8,128)}) %all-reduce.3.cloned.1.call-update) | async-done | bytes 65552 | tf_op jit(solution)/shard_map/psum | solution.py:48
  270.5 1.0 copy.28
  271.5 14.1 %all_gather.3 = f32[256,256]{1,0:T(8,128)S(1)} all-gather(f32[64,256]{1,0:T(8,128)S(1)} %copy.28), channel_id=1, replica_groups=mesh['gx'=4,'gy'=2,'gz'=4] {'gz'}, dimensions={0}, use_global_device_ids=true | all-gather | bytes 327680 | tf_op jit(solution)/shard_map/all_gather | solution.py:49
  285.9 11.7 %cholesky.50 = f32[128,128]{1,0:T(8,128)S(1)} custom-call(f32[128,128]{1,0:T(8,128)S(1)} %cholesky.118), custom_call_target="Cholesky" | custom-call | tf_op jit(solution)/shard_map/jit(cholesky)/cholesky | solution.py:51
  297.7 9.8 %custom-call.14 = f32[1,128,128]{1,2,0:T(8,128)S(1)} custom-call(f32[1,128,128]{2,1,0:T(8,128)S(1)} %get-tuple-element.35), custom_call_target="InvertDiagBlocksLowerTriangular" | custom-call | tf_op jit(solution)/shard_map/jit(cholesky)/cholesky | solution.py:51
  307.7 0.3 convolution_subtract_fusion.1
  308.0 11.7 %cholesky.105 = f32[128,128]{1,0:T(8,128)S(1)} custom-call(f32[128,128]{1,0:T(8,128)S(1)} %convolution_subtract_fusion.1), custom_call_target="Cholesky" | custom-call | tf_op jit(solution)/shard_map/jit(cholesky)/cholesky | solution.py:51
  319.7 0.6 compare_reduce_fusion
  321.7 4.0 %while.1 = (s32[]{:T(128)}, f32[256,256]{1,0:T(8,128)S(1)}, s32[2,2]{1,0:T(2,128)S(1)}, f32[2,128,128]{2,1,0:T(8,128)S(1)}, s32[]{:T(128)}) while((s32[]{:T(128)}, f32[256,256]{1,0:T(8,128)S(1)}, s32[2,2]{1,0:T(2,128)S(1)}, f32[2,128,128]{2,1,0:T(8,128)S(1)}, s32[]{:T(128)}) %tuple.37), condition=%wide.while_cond, body=%wide.while_body.sunk | while | flops 2 | bytes 131181 | solution.py:52
  321.9 0.6 fusion.114
  322.5 1.3 bitcast_dynamic-update-slice_fusion.2
  323.8 0.6 fusion.114
  324.4 1.3 bitcast_dynamic-update-slice_fusion.2
  325.7 19.7 %custom-call.15 = f32[2,128,128]{1,2,0:T(8,128)S(1)} custom-call(f32[2,128,128]{2,1,0:T(8,128)S(1)} %get-tuple-element.9), custom_call_target="InvertDiagBlocksLowerTriangular" | custom-call | tf_op jit(solution)/shard_map/triangular_solve | solution.py:52
  345.4 0.3 fusion.53
  346.0 0.3 fusion.56
  346.3 2.8 convolution_bitcast_fusion
  349.1 0.8 copy.32
  (43 shorter events, 1.7 us)
Async XLA Ops:
  7.2 208.0 %reduce-scatter.4.cloned.1.call-start = ((), (), s32[]{:S(2)}) async-start(), calls=%async_computation.2 | async-start | bytes 327680
  7.2 27.8 %copy-start.4 = (f32[1,1,4,256,256]{4,3,2,1,0:T(8,128)S(1)}, f32[1,1,4,256,256]{4,3,2,1,0:T(8,128)}, u32[]{:S(2)}) copy-start(f32[1,1,4,256,256]{4,3,2,1,0:T(8,128)} %param.3) | copy-start | bytes 3145732
  7.2 27.7 %collective-permute-start = (f32[1,1,4,256,256]{4,3,2,1,0:T(8,128)}, f32[1,1,4,256,256]{4,3,2,1,0:T(8,128)S(1)}, u32[]{:S(2)}, u32[]{:S(2)}) collective-permute-start(f32[1,1,4,256,256]{4,3,2,1,0:T(8,128)} %param.3), channel_id=1, source_target_pairs={{0,8},{8,16},{16,24},{1,9},{9,17},{17,25},{2,10},{10,18},{18,26},{... | collective-permute-start | bytes 3145736 | tf_op jit(solution)/shard_map/ppermute | solution.py:14
  12.3 47.0 %collective-permute-start.1 = (f32[1,1,4,256,256]{4,3,2,1,0:T(8,128)}, f32[1,1,4,256,256]{4,3,2,1,0:T(8,128)S(1)}, u32[]{:S(2)}, u32[]{:S(2)}) collective-permute-start(f32[1,1,4,256,256]{4,3,2,1,0:T(8,128)} %param.3), channel_id=1, source_target_pairs={{8,0},{16,8},{24,16},{9,1},{17,9},{25,17},{10,2},{18,10},{26,18},{... | collective-permute-start | bytes 3145736 | tf_op jit(solution)/shard_map/ppermute | solution.py:15
  59.3 6.6 %collective-permute-start.2 = (f32[3,1,4,256,256]{4,3,2,1,0:T(8,128)S(1)}, f32[3,1,4,256,256]{4,3,2,1,0:T(8,128)S(1)}, u32[]{:S(2)}, u32[]{:S(2)}) collective-permute-start(f32[3,1,4,256,256]{4,3,2,1,0:T(8,128)S(1)} %constant_dynamic-update-slice_fusion), channel_id=1, source_target_pairs={{0,4},{1,5},{2,6},{3,7},{8,12},{9,13},{10,14},{11,15},{16,20},{17,... | collective-permute-start | bytes 9437192 | tf_op jit(solution)/shard_map/ppermute | solution.py:14
  60.8 7.6 %collective-permute-start.3 = (f32[3,1,4,256,256]{4,3,2,1,0:T(8,128)S(1)}, f32[3,1,4,256,256]{4,3,2,1,0:T(8,128)S(1)}, u32[]{:S(2)}, u32[]{:S(2)}) collective-permute-start(f32[3,1,4,256,256]{4,3,2,1,0:T(8,128)S(1)} %constant_dynamic-update-slice_fusion), channel_id=1, source_target_pairs={{4,0},{5,1},{6,2},{7,3},{12,8},{13,9},{14,10},{15,11},{20,16},{21,... | collective-permute-start | bytes 9437192 | tf_op jit(solution)/shard_map/ppermute | solution.py:15
  65.9 5.3 %copy-start = (f32[3,1,4,256,256]{4,3,2,1,0:T(8,128)}, f32[3,1,4,256,256]{4,3,2,1,0:T(8,128)S(1)}, u32[]{:S(2)}) copy-start(f32[3,1,4,256,256]{4,3,2,1,0:T(8,128)S(1)} %collective-permute-done.2) | copy-start | bytes 9437188
  68.4 3.0 copy-start.1
  71.4 12.8 %copy-start.8 = (s32[1,1,4,10]{3,2,1,0:T(4,128)S(1)}, s32[1,1,4,10]{3,2,1,0:T(4,128)}, u32[]{:S(2)}) copy-start(s32[1,1,4,10]{3,2,1,0:T(4,128)} %param.5) | copy-start | bytes 484
  71.4 54.7 %collective-permute-start.4 = (f32[3,3,1,256,256]{4,3,2,1,0:T(8,128)}, f32[3,3,1,256,256]{4,3,2,1,0:T(8,128)}, u32[]{:S(2)}, u32[]{:S(2)}) collective-permute-start(f32[3,3,1,256,256]{4,3,2,1,0:T(8,128)} %get-tuple-element.24), channel_id=1, source_target_pairs={{0,1},{1,2},{2,3},{4,5},{5,6},{6,7},{8,9},{9,10},{10,11},{12,13},{... | collective-permute-start | bytes 7077896 | tf_op jit(solution)/shard_map/ppermute | solution.py:14
  76.4 55.2 %collective-permute-start.5 = (f32[3,3,1,256,256]{4,3,2,1,0:T(8,128)}, f32[3,3,1,256,256]{4,3,2,1,0:T(8,128)}, u32[]{:S(2)}, u32[]{:S(2)}) collective-permute-start(f32[3,3,1,256,256]{4,3,2,1,0:T(8,128)} %get-tuple-element.25), channel_id=1, source_target_pairs={{1,0},{2,1},{3,2},{5,4},{6,5},{7,6},{9,8},{10,9},{11,10},{13,12},{... | collective-permute-start | bytes 7077896 | tf_op jit(solution)/shard_map/ppermute | solution.py:15
  161.7 7.4 %copy-start.7 = (f32[1,1,1,256,256]{3,4,2,1,0:T(8,128)S(1)}, f32[1,1,1,256,256]{3,4,2,1,0:T(8,128)}, u32[]{:S(2)}) copy-start(f32[1,1,1,256,256]{3,4,2,1,0:T(8,128)} %copy.46) | copy-start | bytes 786436
  169.2 7.0 %copy-start.3 = (f32[10,256,256]{2,1,0:T(8,128)S(1)}, f32[10,256,256]{2,1,0:T(8,128)}, u32[]{:S(2)}) copy-start(f32[10,256,256]{2,1,0:T(8,128)} %gather_fusion.2) | copy-start | bytes 7864324
  176.1 6.3 %copy-start.5 = (f32[1,1,1,256,256]{3,4,2,1,0:T(8,128)S(1)}, f32[1,1,1,256,256]{3,4,2,1,0:T(8,128)}, u32[]{:S(2)}) copy-start(f32[1,1,1,256,256]{3,4,2,1,0:T(8,128)} %copy.44) | copy-start | bytes 786436
  182.4 6.7 %copy-start.2 = (f32[10,256,256]{2,1,0:T(8,128)S(1)}, f32[10,256,256]{2,1,0:T(8,128)}, u32[]{:S(2)}) copy-start(f32[10,256,256]{2,1,0:T(8,128)} %gather_fusion) | copy-start | bytes 7864324
  182.4 6.7 %copy-start.6 = (f32[1,1,1,256,256]{3,4,2,1,0:T(8,128)S(1)}, f32[1,1,1,256,256]{3,4,2,1,0:T(8,128)}, u32[]{:S(2)}) copy-start(f32[1,1,1,256,256]{3,4,2,1,0:T(8,128)} %copy.43) | copy-start | bytes 786436
  197.1 73.4 %all-reduce.3.cloned.1.call-start = ((), (), s32[]{:S(2)}) async-start(), calls=%async_computation.1 | async-start | bytes 262144 | tf_op jit(solution)/shard_map/psum | solution.py:48
Sparse Core Ops, SparseCore 0:
  197.2 17.8 reduce-scatter.3
  218.8 51.6 all-reduce.2
where the time goes:
time: 360 us; the launch traced here: 357 us
  waiting for transfers between devices  171 us (48%)
  other arithmetic  66.3 us (18%)
  local copies, waits for them, and re-layouts  42.3 us (12%)
  matrix products  31.9 us (9%)
  between operations  15.8 us (4%)
  starting transfers between devices  15.5 us (4%)
  blocking collectives  14.1 us (4%)
    ppermute x3, waiting for transfers between devices, padded_2(): before = lax.ppermute(last, axis, up)  67 us
    psum x1, waiting for transfers between devices, per_device(): gram_part = lax.psum(gram_part, ('gx', 'gy'))  53.7 us
    another operation x6, other arithmetic, per_device(): lower = jnp.linalg.cholesky(gram)  34 us
    ppermute x3, waiting for transfers between devices, padded_2(): after = lax.ppermute(initial, axis, down)  32.1 us
    gather x4, local copies, waits for them, and re-layouts, window(): lax.dynamic_slice(padded, (first, second, third, zero, zero), (1, 1, 1, p...  27.8 us
    dot_general x4, matrix products, per_device(): jnp.einsum('kab,kbc->ac', tiles[0, 0, element_cell], windows, precision=l...  26.1 us
    another operation x2, other arithmetic, per_device(): lax.linalg.triangular_solve(lower, jnp.eye(width, dtype=gram.dtype), left...  19.7 us
    unnamed x3, waiting for transfers between devices  18 us
  transfers between devices with their start and end apart: 8, of which 8 were waited for; matrix products, arithmetic and copies ran while one was open for 2% of the time, Pallas kernels for 0%

commit v1 on v0

--- a/solution.py
+++ b/solution.py
@@ -45,7 +45,7 @@
     local_gram = jnp.dot(flat_rows.T, flat_rows, precision=lax.Precision.HIGHEST)
     row_total = flat_rows.shape[0] * lax.axis_size("gx") * lax.axis_size("gy") * lax.axis_size("gz")
     gram_part = lax.psum_scatter(local_gram, "gz", scatter_dimension=0, tiled=True)
-    gram_part = lax.psum(gram_part, ("gx", "gy"))
+    gram_part = jnp.sum(lax.all_gather(gram_part, ("gx", "gy")), axis=0)
     summed = lax.all_gather(gram_part, "gz", axis=0, tiled=True)
     gram = summed / row_total
     lower = jnp.linalg.cholesky(gram)

time: 360 us -> 315 us (0.88)
  waiting for transfers between devices: 171 us -> 117 us
  blocking collectives: 14.1 us -> 24.8 us
    psum x1 -> x0, waiting for transfers between devices: 53.7 us -> none  [per_device(): gram_part = lax.psum(gram_part, ('gx', 'gy'))]
    unnamed x3 -> x1, waiting for transfers between devices: 18 us -> 0.02 us
    reduce_scatter x0 -> x1, waiting for transfers between devices: none -> 18 us  [per_device(): lax.psum_scatter(local_gram, 'gz', scatter_dimension=0, tiled=True)]
    all_gather x0 -> x1, blocking collectives: none -> 10.1 us  [per_device(): gram_part = jnp.sum(lax.all_gather(gram_part, ('gx', 'gy')), axis=0)]
    unnamed x26 -> x25, local copies, waits for them, and re-layouts: 8.34 us -> 6.75 us
  transfers between devices with their start and end apart: 8 -> 7, of which waited for: 8 -> 7; matrix products, arithmetic and copies ran while one was open for 2% -> 2% of each run, Pallas kernels for 0% -> 0%
where the time goes in v1:
time: 315 us; the launch traced here: 312 us
  waiting for transfers between devices  117 us (37%)
  other arithmetic  66.4 us (21%)
  local copies, waits for them, and re-layouts  39.9 us (13%)
  matrix products  31.9 us (10%)
  blocking collectives  24.8 us (8%)
  between operations  15.9 us (5%)
  starting transfers between devices  15.5 us (5%)
    ppermute x3, waiting for transfers between devices, padded_2(): before = lax.ppermute(last, axis, up)  67 us
    another operation x6, other arithmetic, per_device(): lower = jnp.linalg.cholesky(gram)  34 us
    ppermute x3, waiting for transfers between devices, padded_2(): after = lax.ppermute(initial, axis, down)  32.1 us
    gather x4, local copies, waits for them, and re-layouts, window(): lax.dynamic_slice(padded, (first, second, third, zero, zero), (1, 1, 1, p...  27.8 us
    dot_general x4, matrix products, per_device(): jnp.einsum('kab,kbc->ac', tiles[0, 0, element_cell], windows, precision=l...  26.1 us
    another operation x2, other arithmetic, per_device(): lax.linalg.triangular_solve(lower, jnp.eye(width, dtype=gram.dtype), left...  19.7 us
    reduce_scatter x1, waiting for transfers between devices, per_device(): lax.psum_scatter(local_gram, 'gz', scatter_dimension=0, tiled=True)  18 us
    all_gather x1, blocking collectives, per_device(): summed = lax.all_gather(gram_part, 'gz', axis=0, tiled=True)  14.7 us
  transfers between devices with their start and end apart: 7, of which 7 were waited for; matrix products, arithmetic and copies ran while one was open for 2% of the time, Pallas kernels for 0%

profile of v1, /device:TPU:0, one launch (start us, length us, event | category | flops | bytes accessed | tf_op | source)
XLA Modules:
  0.0 311.7 jit_solution(11853047440970672563)
XLA Ops:
  7.2 5.1 %collective-permute-start = (f32[1,1,4,256,256]{4,3,2,1,0:T(8,128)}, f32[1,1,4,256,256]{4,3,2,1,0:T(8,128)S(1)}, u32[]{:S(2)}, u32[]{:S(2)}) collective-permute-start(f32[1,1,4,256,256]{4,3,2,1,0:T(8,128)} %param.3), channel_id=1, source_target_pairs={{0,8},{8,16},{16,24},{1,9},{9,17},{17,25},{2,10},{10,18},{18,26},{... | collective-permute-start | bytes 3145736 | tf_op jit(solution)/shard_map/ppermute | solution.py:14
  12.3 1.3 collective-permute-start.1
  13.6 21.3 %collective-permute-done = f32[1,1,4,256,256]{4,3,2,1,0:T(8,128)S(1)} collective-permute-done((f32[1,1,4,256,256]{4,3,2,1,0:T(8,128)}, f32[1,1,4,256,256]{4,3,2,1,0:T(8,128)S(1)}, u32[]{:S(2)}, u32[]{:S(2)}) %collective-permute-start) | collective-permute-done | bytes 1048608 | tf_op jit(solution)/shard_map/ppermute | solution.py:14
  35.1 24.1 %collective-permute-done.1 = f32[1,1,4,256,256]{4,3,2,1,0:T(8,128)S(1)} collective-permute-done((f32[1,1,4,256,256]{4,3,2,1,0:T(8,128)}, f32[1,1,4,256,256]{4,3,2,1,0:T(8,128)S(1)}, u32[]{:S(2)}, u32[]{:S(2)}) %collective-permute-start.1) | collective-permute-done | bytes 1048608 | tf_op jit(solution)/shard_map/ppermute | solution.py:15
  59.3 1.5 collective-permute-start.2
  60.8 1.3 collective-permute-start.3
  62.1 3.8 %collective-permute-done.2 = f32[3,1,4,256,256]{4,3,2,1,0:T(8,128)S(1)} collective-permute-done((f32[3,1,4,256,256]{4,3,2,1,0:T(8,128)S(1)}, f32[3,1,4,256,256]{4,3,2,1,0:T(8,128)S(1)}, u32[]{:S(2)}, u32[]{:S(2)}) %collective-permute-start.2) | collective-permute-done | bytes 3145760 | tf_op jit(solution)/shard_map/ppermute | solution.py:14
  65.9 2.5 collective-permute-done.3
  68.4 2.8 pad_maximum_fusion.3
  71.4 5.0 %collective-permute-start.4 = (f32[3,3,1,256,256]{4,3,2,1,0:T(8,128)}, f32[3,3,1,256,256]{4,3,2,1,0:T(8,128)}, u32[]{:S(2)}, u32[]{:S(2)}) collective-permute-start(f32[3,3,1,256,256]{4,3,2,1,0:T(8,128)} %get-tuple-element.24), channel_id=1, source_target_pairs={{0,1},{1,2},{2,3},{4,5},{5,6},{6,7},{8,9},{9,10},{10,11},{12,13},{... | collective-permute-start | bytes 7077896 | tf_op jit(solution)/shard_map/ppermute | solution.py:14
  76.5 1.3 collective-permute-start.5
  77.7 0.9 fusion.104
  78.7 0.8 copy.39
  79.5 1.1 copy.38
  80.6 1.8 copy.37
  82.4 1.8 copy.36
  84.3 41.9 %collective-permute-done.4 = f32[3,3,1,256,256]{4,3,2,1,0:T(8,128)} collective-permute-done((f32[3,3,1,256,256]{4,3,2,1,0:T(8,128)}, f32[3,3,1,256,256]{4,3,2,1,0:T(8,128)}, u32[]{:S(2)}, u32[]{:S(2)}) %collective-permute-start.4) | collective-permute-done | bytes 2359328 | tf_op jit(solution)/shard_map/ppermute | solution.py:14
  126.1 5.5 %collective-permute-done.5 = f32[3,3,1,256,256]{4,3,2,1,0:T(8,128)} collective-permute-done((f32[3,3,1,256,256]{4,3,2,1,0:T(8,128)}, f32[3,3,1,256,256]{4,3,2,1,0:T(8,128)}, u32[]{:S(2)}, u32[]{:S(2)}) %collective-permute-start.5) | collective-permute-done | bytes 2359328 | tf_op jit(solution)/shard_map/ppermute | solution.py:15
  131.7 9.7 %pad_maximum_fusion = f32[3,3,6,256,256]{4,3,2,1,0:T(8,128)} fusion(f32[3,3,1,256,256]{4,3,2,1,0:T(8,128)} %collective-permute-done.5, f32[3,1,4,256,256]{4,3,2,1,0:T(8,128)} %copy-done.1, f32[3,1,4,256,256]{4,3,2,1,0:T(8,128)S(1)} %constant_dynamic-update-slice_fusion, f32[3,1,4,256,256]{4,3,2,1,0:T(8,128)} %copy-done, ...), kind=kLoop, calls=%fused_computation.6 | loop fusion | flops 14155776 | bytes 28311552 | tf_op jit(solution)/shard_map/concatenate | solution.py:16
  141.4 7.3 %gather_fusion.3 = f32[10,256,256]{2,1,0:T(8,128)} fusion(f32[3,3,6,256,256]{4,3,2,1,0:T(8,128)} %pad_maximum_fusion, s32[10]{0:T(128)S(1)} %get-tuple-element.38), kind=kCustom, calls=%fused_computation.3 | custom fusion | bytes 5243080 | tf_op jit(solution)/shard_map/vmap()/gather | solution.py:22
  148.7 7.4 %gather_fusion.2 = f32[10,256,256]{2,1,0:T(8,128)} fusion(f32[3,3,6,256,256]{4,3,2,1,0:T(8,128)} %pad_maximum_fusion, s32[10]{0:T(128)S(1)} %get-tuple-element.39), kind=kCustom, calls=%fused_computation.2 | custom fusion | bytes 5243080 | tf_op jit(solution)/shard_map/vmap()/gather | solution.py:22
  156.0 5.7 %gather_fusion.1 = f32[10,256,256]{2,1,0:T(8,128)S(1)} fusion(f32[3,3,6,256,256]{4,3,2,1,0:T(8,128)} %pad_maximum_fusion, s32[10]{0:T(128)S(1)} %get-tuple-element.37), kind=kCustom, calls=%fused_computation.1 | custom fusion | bytes 5243080 | tf_op jit(solution)/shard_map/vmap()/gather | solution.py:22
  161.8 7.4 %gather_fusion = f32[10,256,256]{2,1,0:T(8,128)} fusion(f32[3,3,6,256,256]{4,3,2,1,0:T(8,128)} %pad_maximum_fusion, s32[10]{0:T(128)S(1)} %get-tuple-element.36), kind=kCustom, calls=%fused_computation | custom fusion | bytes 5243080 | tf_op jit(solution)/shard_map/vmap()/gather | solution.py:22
  169.2 7.0 %fusion.27 = f32[1,256,256]{1,2,0:T(8,128)S(1)} fusion(f32[10,256,256]{2,1,0:T(8,128)} %gather_fusion.3, f32[1,1,4,10,256,256]{5,4,3,2,1,0:T(8,128)} %param.4, f32[1,1,1,256,256]{3,4,2,1,0:T(8,128)S(1)} %copy-done.7), kind=kOutput, calls=%fused_computation.29 | convolution fusion | flops 2013396992 | bytes 5767168 | tf_op jit(solution)/shard_map/kab,kbc->ac/dot_general | solution.py:39
  176.2 6.2 %fusion.33 = f32[1,256,256]{1,2,0:T(8,128)S(1)} fusion(f32[10,256,256]{2,1,0:T(8,128)S(1)} %copy-done.3, f32[1,1,4,10,256,256]{5,4,3,2,1,0:T(8,128)} %param.4, f32[1,1,1,256,256]{3,4,2,1,0:T(8,128)S(1)} %copy.38), kind=kOutput, calls=%fused_computation.31 | convolution fusion | flops 2013396992 | bytes 5767168 | tf_op jit(solution)/shard_map/kab,kbc->ac/dot_general | solution.py:39
  182.5 6.7 %fusion.39 = f32[1,256,256]{1,2,0:T(8,128)S(1)} fusion(f32[10,256,256]{2,1,0:T(8,128)S(1)} %gather_fusion.1, f32[1,1,4,10,256,256]{5,4,3,2,1,0:T(8,128)} %param.4, f32[1,1,1,256,256]{3,4,2,1,0:T(8,128)S(1)} %copy-done.5), kind=kOutput, calls=%fused_computation.33 | convolution fusion | flops 2013396992 | bytes 5767168 | tf_op jit(solution)/shard_map/kab,kbc->ac/dot_general | solution.py:39
  189.2 6.2 %fusion.45 = f32[1,256,256]{1,2,0:T(8,128)S(1)} fusion(f32[10,256,256]{2,1,0:T(8,128)S(1)} %copy-done.2, f32[1,1,4,10,256,256]{5,4,3,2,1,0:T(8,128)} %param.4, f32[1,1,1,256,256]{3,4,2,1,0:T(8,128)S(1)} %copy-done.6), kind=kOutput, calls=%fused_computation.35 | convolution fusion | flops 2013396992 | bytes 5767168 | tf_op jit(solution)/shard_map/kab,kbc->ac/dot_general | solution.py:39
  195.4 1.7 convolution_bitcast_fusion.1
  197.2 18.0 %reduce-scatter.2.cloned.1.call-done = f32[64,256]{1,0:T(8,128)} async-done(((f32[256,256]{1,0:T(8,128)}), f32[64,256]{1,0:T(8,128)}) %reduce-scatter.2.cloned.1.call-update) | async-done | bytes 65552 | tf_op jit(solution)/shard_map/reduce_scatter | solution.py:47
  215.2 10.1 %all-gather = f32[512,256]{1,0:T(8,128)S(1)} all-gather(f32[64,256]{1,0:T(8,128)} %reduce-scatter.2.cloned.1.call-done), channel_id=2, replica_groups=mesh['gx'=4,'gy'=2,'gz'=4] {'gx','gy'}, dimensions={0}, use_global_device_ids=true | all-gather | bytes 589824 | tf_op jit(solution)/shard_map/all_gather | solution.py:48
  225.3 14.7 %all_gather.11 = f32[256,256]{1,0:T(8,128)S(1)} all-gather(f32[64,256]{1,0:T(8,128)S(1)} %reduce_sum.9), channel_id=1, replica_groups=mesh['gx'=4,'gy'=2,'gz'=4] {'gz'}, dimensions={0}, use_global_device_ids=true | all-gather | bytes 327680 | tf_op jit(solution)/shard_map/all_gather | solution.py:49
  240.4 11.7 %cholesky.50 = f32[128,128]{1,0:T(8,128)S(1)} custom-call(f32[128,128]{1,0:T(8,128)S(1)} %cholesky.118), custom_call_target="Cholesky" | custom-call | tf_op jit(solution)/shard_map/jit(cholesky)/cholesky | solution.py:51
  252.2 9.8 %custom-call.14 = f32[1,128,128]{1,2,0:T(8,128)S(1)} custom-call(f32[1,128,128]{2,1,0:T(8,128)S(1)} %get-tuple-element.35), custom_call_target="InvertDiagBlocksLowerTriangular" | custom-call | tf_op jit(solution)/shard_map/jit(cholesky)/cholesky | solution.py:51
  262.0 0.2 constant_dynamic-update-slice_fusion.4
  262.2 0.3 convolution_subtract_fusion.1
  262.5 11.7 %cholesky.105 = f32[128,128]{1,0:T(8,128)S(1)} custom-call(f32[128,128]{1,0:T(8,128)S(1)} %convolution_subtract_fusion.1), custom_call_target="Cholesky" | custom-call | tf_op jit(solution)/shard_map/jit(cholesky)/cholesky | solution.py:51
  274.2 0.7 compare_reduce_fusion
  276.3 4.2 %while.1 = (s32[]{:T(128)}, f32[256,256]{1,0:T(8,128)S(1)}, s32[2,2]{1,0:T(2,128)S(1)}, f32[2,128,128]{2,1,0:T(8,128)S(1)}, s32[]{:T(128)}) while((s32[]{:T(128)}, f32[256,256]{1,0:T(8,128)S(1)}, s32[2,2]{1,0:T(2,128)S(1)}, f32[2,128,128]{2,1,0:T(8,128)S(1)}, s32[]{:T(128)}) %tuple.37), condition=%wide.while_cond, body=%wide.while_body.sunk | while | flops 2 | bytes 131181 | solution.py:52
  276.5 0.6 fusion.114
  277.1 1.4 bitcast_dynamic-update-slice_fusion.2
  278.5 0.6 fusion.114
  279.1 1.4 bitcast_dynamic-update-slice_fusion.2
  280.5 19.7 %custom-call.15 = f32[2,128,128]{1,2,0:T(8,128)S(1)} custom-call(f32[2,128,128]{2,1,0:T(8,128)S(1)} %get-tuple-element.9), custom_call_target="InvertDiagBlocksLowerTriangular" | custom-call | tf_op jit(solution)/shard_map/triangular_solve | solution.py:52
  300.1 0.3 fusion.53
  300.4 0.3 convolution_subtract_fusion
  300.7 0.3 fusion.56
  301.0 2.8 convolution_bitcast_fusion
  303.8 0.8 copy.29
  (40 shorter events, 1.2 us)
Async XLA Ops:
  7.2 208.0 %reduce-scatter.2.cloned.1.call-start = ((), (), s32[]{:S(2)}) async-start(), calls=%async_computation.1 | async-start | bytes 327680 | tf_op jit(solution)/shard_map/reduce_scatter | solution.py:47
  7.2 27.8 %copy-start.4 = (f32[1,1,4,256,256]{4,3,2,1,0:T(8,128)S(1)}, f32[1,1,4,256,256]{4,3,2,1,0:T(8,128)}, u32[]{:S(2)}) copy-start(f32[1,1,4,256,256]{4,3,2,1,0:T(8,128)} %param.3) | copy-start | bytes 3145732
  7.2 27.7 %collective-permute-start = (f32[1,1,4,256,256]{4,3,2,1,0:T(8,128)}, f32[1,1,4,256,256]{4,3,2,1,0:T(8,128)S(1)}, u32[]{:S(2)}, u32[]{:S(2)}) collective-permute-start(f32[1,1,4,256,256]{4,3,2,1,0:T(8,128)} %param.3), channel_id=1, source_target_pairs={{0,8},{8,16},{16,24},{1,9},{9,17},{17,25},{2,10},{10,18},{18,26},{... | collective-permute-start | bytes 3145736 | tf_op jit(solution)/shard_map/ppermute | solution.py:14
  12.3 47.0 %collective-permute-start.1 = (f32[1,1,4,256,256]{4,3,2,1,0:T(8,128)}, f32[1,1,4,256,256]{4,3,2,1,0:T(8,128)S(1)}, u32[]{:S(2)}, u32[]{:S(2)}) collective-permute-start(f32[1,1,4,256,256]{4,3,2,1,0:T(8,128)} %param.3), channel_id=1, source_target_pairs={{8,0},{16,8},{24,16},{9,1},{17,9},{25,17},{10,2},{18,10},{26,18},{... | collective-permute-start | bytes 3145736 | tf_op jit(solution)/shard_map/ppermute | solution.py:15
  59.3 6.6 %collective-permute-start.2 = (f32[3,1,4,256,256]{4,3,2,1,0:T(8,128)S(1)}, f32[3,1,4,256,256]{4,3,2,1,0:T(8,128)S(1)}, u32[]{:S(2)}, u32[]{:S(2)}) collective-permute-start(f32[3,1,4,256,256]{4,3,2,1,0:T(8,128)S(1)} %constant_dynamic-update-slice_fusion), channel_id=1, source_target_pairs={{0,4},{1,5},{2,6},{3,7},{8,12},{9,13},{10,14},{11,15},{16,20},{17,... | collective-permute-start | bytes 9437192 | tf_op jit(solution)/shard_map/ppermute | solution.py:14
  60.8 7.6 %collective-permute-start.3 = (f32[3,1,4,256,256]{4,3,2,1,0:T(8,128)S(1)}, f32[3,1,4,256,256]{4,3,2,1,0:T(8,128)S(1)}, u32[]{:S(2)}, u32[]{:S(2)}) collective-permute-start(f32[3,1,4,256,256]{4,3,2,1,0:T(8,128)S(1)} %constant_dynamic-update-slice_fusion), channel_id=1, source_target_pairs={{4,0},{5,1},{6,2},{7,3},{12,8},{13,9},{14,10},{15,11},{20,16},{21,... | collective-permute-start | bytes 9437192 | tf_op jit(solution)/shard_map/ppermute | solution.py:15
  65.9 5.3 %copy-start = (f32[3,1,4,256,256]{4,3,2,1,0:T(8,128)}, f32[3,1,4,256,256]{4,3,2,1,0:T(8,128)S(1)}, u32[]{:S(2)}) copy-start(f32[3,1,4,256,256]{4,3,2,1,0:T(8,128)S(1)} %collective-permute-done.2) | copy-start | bytes 9437188
  68.4 3.0 copy-start.1
  71.4 12.8 %copy-start.8 = (s32[1,1,4,10]{3,2,1,0:T(4,128)S(1)}, s32[1,1,4,10]{3,2,1,0:T(4,128)}, u32[]{:S(2)}) copy-start(s32[1,1,4,10]{3,2,1,0:T(4,128)} %param.5) | copy-start | bytes 484
  71.4 54.7 %collective-permute-start.4 = (f32[3,3,1,256,256]{4,3,2,1,0:T(8,128)}, f32[3,3,1,256,256]{4,3,2,1,0:T(8,128)}, u32[]{:S(2)}, u32[]{:S(2)}) collective-permute-start(f32[3,3,1,256,256]{4,3,2,1,0:T(8,128)} %get-tuple-element.24), channel_id=1, source_target_pairs={{0,1},{1,2},{2,3},{4,5},{5,6},{6,7},{8,9},{9,10},{10,11},{12,13},{... | collective-permute-start | bytes 7077896 | tf_op jit(solution)/shard_map/ppermute | solution.py:14
  76.5 55.2 %collective-permute-start.5 = (f32[3,3,1,256,256]{4,3,2,1,0:T(8,128)}, f32[3,3,1,256,256]{4,3,2,1,0:T(8,128)}, u32[]{:S(2)}, u32[]{:S(2)}) collective-permute-start(f32[3,3,1,256,256]{4,3,2,1,0:T(8,128)} %get-tuple-element.25), channel_id=1, source_target_pairs={{1,0},{2,1},{3,2},{5,4},{6,5},{7,6},{9,8},{10,9},{11,10},{13,12},{... | collective-permute-start | bytes 7077896 | tf_op jit(solution)/shard_map/ppermute | solution.py:15
  161.8 7.4 %copy-start.7 = (f32[1,1,1,256,256]{3,4,2,1,0:T(8,128)S(1)}, f32[1,1,1,256,256]{3,4,2,1,0:T(8,128)}, u32[]{:S(2)}) copy-start(f32[1,1,1,256,256]{3,4,2,1,0:T(8,128)} %copy.39) | copy-start | bytes 786436
  169.2 7.0 %copy-start.3 = (f32[10,256,256]{2,1,0:T(8,128)S(1)}, f32[10,256,256]{2,1,0:T(8,128)}, u32[]{:S(2)}) copy-start(f32[10,256,256]{2,1,0:T(8,128)} %gather_fusion.2) | copy-start | bytes 7864324
  176.2 6.3 %copy-start.5 = (f32[1,1,1,256,256]{3,4,2,1,0:T(8,128)S(1)}, f32[1,1,1,256,256]{3,4,2,1,0:T(8,128)}, u32[]{:S(2)}) copy-start(f32[1,1,1,256,256]{3,4,2,1,0:T(8,128)} %copy.37) | copy-start | bytes 786436
  182.5 6.7 %copy-start.2 = (f32[10,256,256]{2,1,0:T(8,128)S(1)}, f32[10,256,256]{2,1,0:T(8,128)}, u32[]{:S(2)}) copy-start(f32[10,256,256]{2,1,0:T(8,128)} %gather_fusion) | copy-start | bytes 7864324
  182.5 6.7 %copy-start.6 = (f32[1,1,1,256,256]{3,4,2,1,0:T(8,128)S(1)}, f32[1,1,1,256,256]{3,4,2,1,0:T(8,128)}, u32[]{:S(2)}) copy-start(f32[1,1,1,256,256]{3,4,2,1,0:T(8,128)} %copy.36) | copy-start | bytes 786436
Sparse Core Ops, SparseCore 0:
  197.3 17.8 reduce-scatter.1
